TPU v7x, 32 devices: a whole 2x2x4 slice. The times are simulated.
32 devices in a mesh: dp: 8 (over y, x, core), seq: 4 (over z).
Axes of the slice: x: 2, y: 2, z: 4, core: 2. Of those that a mesh axis runs over, the one named last changes fastest.
Arguments:
- inputs: bfloat16 [24, 1024, 768], P('dp', 'seq'), may hold values from -6 to 6
- segment_ids: int32 [24, 1024], P('dp', 'seq'), may hold values from 0 to 3, never falling along the last dimension, each value on 1 to 512 neighbouring positions
- norm1_gain: bfloat16 [768], P('dp'), may hold values from 0.5 to 1.5
- norm1_shift: bfloat16 [768], P('dp'), may hold values from -1.5 to 1.5
- query_weight: bfloat16 [768, 768], P('dp'), may hold values from -0.4375 to 0.4375
- query_bias: bfloat16 [768], P('dp'), may hold values from -2.5 to 2.5
- key_weight: bfloat16 [768, 768], P('dp'), may hold values from -0.21875 to 0.21875
- value_weight: bfloat16 [768, 768], P('dp'), may hold values from -0.21875 to 0.21875
- value_bias: bfloat16 [768], P('dp'), may hold values from -1.5 to 1.5
- out_weight: bfloat16 [768, 768], P('dp'), may hold values from -0.625 to 0.625
- out_bias: bfloat16 [768], P('dp'), may hold values from -1.5 to 1.5
- norm2_gain: bfloat16 [768], P('dp'), may hold values from 0.5 to 1.5
- norm2_shift: bfloat16 [768], P('dp'), may hold values from -1.5 to 1.5
- fc1_weight: bfloat16 [768, 3072], P('dp'), may hold values from -0.21875 to 0.21875
- fc1_bias: bfloat16 [3072], P('dp'), may hold values from -1.5 to 1.5
- fc2_weight: bfloat16 [3072, 768], P('dp'), may hold values from -0.15625 to 0.15625
- fc2_bias: bfloat16 [768], P('dp'), may hold values from -1.5 to 1.5
- grad_output: bfloat16 [24, 1024, 768], P('dp', 'seq'), may hold values from -6 to 6
Outputs:
- output: bfloat16 [24, 1024, 768], P('dp', 'seq')
- grad_inputs: bfloat16 [24, 1024, 768], P('dp', 'seq')
- grad_norm1_gain: float32 [768], P('dp')
- grad_norm1_shift: float32 [768], P('dp')
- grad_query_weight: float32 [768, 768], P('dp')
- grad_query_bias: float32 [768], P('dp')
- grad_key_weight: float32 [768, 768], P('dp')
- grad_value_weight: float32 [768, 768], P('dp')
- grad_value_bias: float32 [768], P('dp')
- grad_out_weight: float32 [768, 768], P('dp')
- grad_out_bias: float32 [768], P('dp')
- grad_norm2_gain: float32 [768], P('dp')
- grad_norm2_shift: float32 [768], P('dp')
- grad_fc1_weight: float32 [768, 3072], P('dp')
- grad_fc1_bias: float32 [3072], P('dp')
- grad_fc2_weight: float32 [3072, 768], P('dp')
- grad_fc2_bias: float32 [768], P('dp')
Inputs may be any that keep to these rules, and one draw needn't show every extreme that they name: `segment_ids`: within each sequence, segment numbers never fall along the positions; each segment is a run of 1 to 512 positions.
All inputs are finite; a program needn't handle non-finite values.
Results may differ from a plain program's by a relative error of at most 0.017.
Values may be sent and summed in bfloat16 or wider, within the bound.
No kernel may reach another device: no remote copies, remote signals or barrier semaphores. Data moves between devices by JAX's collectives and lax.ppermute only.
A program may use at most 192 MiB of HBM per device.

v0:
```python
import jax
import jax.numpy as jnp
from jax import lax
from jax.sharding import PartitionSpec as P

HD = 64
EPSILON = 1e-05


def layer_norm(values, gain, shift):
    center = values - jnp.mean(values, axis=-1, keepdims=True)
    inverse = lax.rsqrt(jnp.mean(center * center, axis=-1, keepdims=True) + EPSILON)
    normed = center * inverse
    return (normed * gain + shift, normed, inverse)


def norm_back(grad, normed, inverse, gain):
    scaled = grad * gain
    return inverse * (
        scaled
        - jnp.mean(scaled, axis=-1, keepdims=True)
        - normed * jnp.mean(scaled * normed, axis=-1, keepdims=True)
    )


def gelu_slope(pre_act):
    return (
        0.5 * (1.0 + lax.erf(pre_act * 0.7071067811865476))
        + pre_act * jnp.exp(-0.5 * pre_act * pre_act) * 0.3989422804014327
    )


def cross_rows(left, right):
    return lax.dot_general(
        left, right, (((0,), (0,)), ((), ())), preferred_element_type=jnp.float32
    )


def times_transpose(left, right):
    return lax.dot_general(
        left, right, (((1,), (1,)), ((), ())), preferred_element_type=jnp.float32
    )


def to_pairs(array, heads_here):
    seqs_here, positions, _ = array.shape
    shaped = array.reshape(seqs_here, positions, heads_here, HD).transpose(0, 2, 1, 3)
    return shaped.reshape(seqs_here * heads_here, positions, HD)


def from_pairs(array, seqs_here, heads_here):
    positions = array.shape[1]
    shaped = array.reshape(seqs_here, heads_here, positions, HD).transpose(0, 2, 1, 3)
    return shaped.reshape(seqs_here, positions, heads_here * HD)


def masked_scores(query_pair, key_pair, segment_row):
    scores = jnp.einsum(
        "qd,kd->qk", query_pair, key_pair, preferred_element_type=jnp.float32
    ) * HD ** (-0.5)
    same_segment = segment_row[:, None] == segment_row[None, :]
    return jnp.where(same_segment, scores, -1e30)


def attend_forward(packed):
    query_pair, key_pair, value_pair, segment_row = packed
    scores = masked_scores(query_pair, key_pair, segment_row)
    highest = jnp.max(scores, axis=-1, keepdims=True)
    expon = jnp.exp(scores - highest)
    totals = jnp.sum(expon, axis=-1, keepdims=True)
    probs = (expon / totals).astype(jnp.bfloat16)
    result = jnp.dot(probs, value_pair, preferred_element_type=jnp.float32).astype(jnp.bfloat16)
    return (result, (highest + jnp.log(totals))[:, 0])


def attend_backward(packed):
    query_pair, key_pair, value_pair, segment_row, logsum, grad_pair = packed
    scores = masked_scores(query_pair, key_pair, segment_row)
    probs = jnp.exp(scores - logsum[:, None])
    grad_probs = jnp.einsum("qd,kd->qk", grad_pair, value_pair, preferred_element_type=jnp.float32)
    delta = jnp.sum(probs * grad_probs, axis=-1, keepdims=True)
    grad_scores = (probs * (grad_probs - delta)).astype(jnp.bfloat16)
    factor = HD ** (-0.5)
    grad_query = (
        jnp.einsum("qk,kd->qd", grad_scores, key_pair, preferred_element_type=jnp.float32) * factor
    ).astype(jnp.bfloat16)
    grad_key = (
        jnp.einsum("qk,qd->kd", grad_scores, query_pair, preferred_element_type=jnp.float32)
        * factor
    ).astype(jnp.bfloat16)
    grad_value = jnp.einsum(
        "qk,qd->kd", probs.astype(jnp.bfloat16), grad_pair, preferred_element_type=jnp.float32
    ).astype(jnp.bfloat16)
    return (grad_query, grad_key, grad_value)


def column_sum(array):
    return jnp.sum(array.astype(jnp.float32), axis=0)


def per_device(
    inputs,
    segment_ids,
    norm1_gain,
    norm1_shift,
    query_weight,
    query_bias,
    key_weight,
    value_weight,
    value_bias,
    out_weight,
    out_bias,
    norm2_gain,
    norm2_shift,
    fc1_weight,
    fc1_bias,
    fc2_weight,
    fc2_bias,
    grad_output,
):
    seqs_here, positions, model_width = inputs.shape
    token_rows = seqs_here * positions
    (
        first_gain,
        first_shift,
        w_query,
        b_query,
        w_key,
        w_value,
        b_value,
        w_out,
        b_out,
        second_gain,
        second_shift,
        w_up,
        b_up,
        w_down,
        b_down,
    ) = (
        lax.all_gather(norm1_gain, "dp", axis=0, tiled=True),
        lax.all_gather(norm1_shift, "dp", axis=0, tiled=True),
        lax.all_gather(query_weight, "dp", axis=0, tiled=True),
        lax.all_gather(query_bias, "dp", axis=0, tiled=True),
        lax.all_gather(key_weight, "dp", axis=0, tiled=True),
        lax.all_gather(value_weight, "dp", axis=0, tiled=True),
        lax.all_gather(value_bias, "dp", axis=0, tiled=True),
        lax.all_gather(out_weight, "dp", axis=0, tiled=True),
        lax.all_gather(out_bias, "dp", axis=0, tiled=True),
        lax.all_gather(norm2_gain, "dp", axis=0, tiled=True),
        lax.all_gather(norm2_shift, "dp", axis=0, tiled=True),
        lax.all_gather(fc1_weight, "dp", axis=0, tiled=True),
        lax.all_gather(fc1_bias, "dp", axis=0, tiled=True),
        lax.all_gather(fc2_weight, "dp", axis=0, tiled=True),
        lax.all_gather(fc2_bias, "dp", axis=0, tiled=True),
    )
    full_segments = lax.all_gather(segment_ids, "seq", axis=1, tiled=True)
    flat_in = inputs.reshape(token_rows, model_width).astype(jnp.float32)
    normed_one, unit_one, inverse_one = layer_norm(
        flat_in, first_gain.astype(jnp.float32), first_shift.astype(jnp.float32)
    )
    act_one = normed_one.astype(jnp.bfloat16)
    query_tok = (
        jnp.dot(act_one, w_query, preferred_element_type=jnp.float32) + b_query.astype(jnp.float32)
    ).astype(jnp.bfloat16)
    key_tok = jnp.dot(act_one, w_key, preferred_element_type=jnp.float32).astype(jnp.bfloat16)
    value_tok = (
        jnp.dot(act_one, w_value, preferred_element_type=jnp.float32) + b_value.astype(jnp.float32)
    ).astype(jnp.bfloat16)
    query_heads, key_heads, value_heads = (
        lax.all_to_all(
            query_tok.reshape(seqs_here, positions, model_width),
            "seq",
            split_axis=2,
            concat_axis=1,
            tiled=True,
        ),
        lax.all_to_all(
            key_tok.reshape(seqs_here, positions, model_width),
            "seq",
            split_axis=2,
            concat_axis=1,
            tiled=True,
        ),
        lax.all_to_all(
            value_tok.reshape(seqs_here, positions, model_width),
            "seq",
            split_axis=2,
            concat_axis=1,
            tiled=True,
        ),
    )
    heads_here = query_heads.shape[2] // HD
    query_pairs = to_pairs(query_heads, heads_here)
    key_pairs = to_pairs(key_heads, heads_here)
    value_pairs = to_pairs(value_heads, heads_here)
    segment_pairs = jnp.repeat(full_segments, heads_here, axis=0)
    attn_pairs, logsum = lax.map(
        attend_forward, (query_pairs, key_pairs, value_pairs, segment_pairs)
    )
    attn_heads = from_pairs(attn_pairs, seqs_here, heads_here)
    attn_tok = lax.all_to_all(attn_heads, "seq", split_axis=1, concat_axis=2, tiled=True).reshape(
        token_rows, model_width
    )
    middle = (
        flat_in
        + jnp.dot(attn_tok, w_out, preferred_element_type=jnp.float32)
        + b_out.astype(jnp.float32)
    )
    normed_two, unit_two, inverse_two = layer_norm(
        middle, second_gain.astype(jnp.float32), second_shift.astype(jnp.float32)
    )
    act_two = normed_two.astype(jnp.bfloat16)
    pre_act = jnp.dot(act_two, w_up, preferred_element_type=jnp.float32) + b_up.astype(jnp.float32)
    hidden = jax.nn.gelu(pre_act, approximate=False).astype(jnp.bfloat16)
    result = (
        middle
        + jnp.dot(hidden, w_down, preferred_element_type=jnp.float32)
        + b_down.astype(jnp.float32)
    )
    output = result.astype(jnp.bfloat16).reshape(seqs_here, positions, model_width)
    first_gain_b, w_query_b, w_key_b, w_value_b, w_out_b, second_gain_b, w_up_b, w_down_b = (
        lax.all_gather(norm1_gain, "dp", axis=0, tiled=True),
        lax.all_gather(query_weight, "dp", axis=0, tiled=True),
        lax.all_gather(key_weight, "dp", axis=0, tiled=True),
        lax.all_gather(value_weight, "dp", axis=0, tiled=True),
        lax.all_gather(out_weight, "dp", axis=0, tiled=True),
        lax.all_gather(norm2_gain, "dp", axis=0, tiled=True),
        lax.all_gather(fc1_weight, "dp", axis=0, tiled=True),
        lax.all_gather(fc2_weight, "dp", axis=0, tiled=True),
    )
    grad_down = grad_output.reshape(token_rows, model_width)
    d_b_down = column_sum(grad_down)
    d_w_down = cross_rows(hidden, grad_down)
    grad_hidden = times_transpose(grad_down, w_down_b)
    grad_pre = (grad_hidden * gelu_slope(pre_act)).astype(jnp.bfloat16)
    d_b_up = column_sum(grad_pre)
    d_w_up = cross_rows(act_two, grad_pre)
    grad_two = times_transpose(grad_pre, w_up_b)
    d_second_gain = jnp.sum(grad_two * unit_two, axis=0)
    d_second_shift = jnp.sum(grad_two, axis=0)
    grad_middle = grad_down.astype(jnp.float32) + norm_back(
        grad_two, unit_two, inverse_two, second_gain_b.astype(jnp.float32)
    )
    grad_branch = grad_middle.astype(jnp.bfloat16)
    d_b_out = column_sum(grad_branch)
    d_w_out = cross_rows(attn_tok, grad_branch)
    grad_attn = (
        times_transpose(grad_branch, w_out_b)
        .astype(jnp.bfloat16)
        .reshape(seqs_here, positions, model_width)
    )
    grad_attn_heads = lax.all_to_all(grad_attn, "seq", split_axis=2, concat_axis=1, tiled=True)
    grad_query_pairs, grad_key_pairs, grad_value_pairs = lax.map(
        attend_backward,
        (
            query_pairs,
            key_pairs,
            value_pairs,
            segment_pairs,
            logsum,
            to_pairs(grad_attn_heads, heads_here),
        ),
    )
    grad_query_tok, grad_key_tok, grad_value_tok = (
        lax.all_to_all(
            from_pairs(grad_query_pairs, seqs_here, heads_here),
            "seq",
            split_axis=1,
            concat_axis=2,
            tiled=True,
        ),
        lax.all_to_all(
            from_pairs(grad_key_pairs, seqs_here, heads_here),
            "seq",
            split_axis=1,
            concat_axis=2,
            tiled=True,
        ),
        lax.all_to_all(
            from_pairs(grad_value_pairs, seqs_here, heads_here),
            "seq",
            split_axis=1,
            concat_axis=2,
            tiled=True,
        ),
    )
    grad_query_tok = grad_query_tok.reshape(token_rows, model_width)
    grad_key_tok = grad_key_tok.reshape(token_rows, model_width)
    grad_value_tok = grad_value_tok.reshape(token_rows, model_width)
    d_b_query = column_sum(grad_query_tok)
    d_b_value = column_sum(grad_value_tok)
    d_w_query = cross_rows(act_one, grad_query_tok)
    d_w_key = cross_rows(act_one, grad_key_tok)
    d_w_value = cross_rows(act_one, grad_value_tok)
    grad_one = (
        times_transpose(grad_query_tok, w_query_b)
        + times_transpose(grad_key_tok, w_key_b)
        + times_transpose(grad_value_tok, w_value_b)
    )
    d_first_gain = jnp.sum(grad_one * unit_one, axis=0)
    d_first_shift = jnp.sum(grad_one, axis=0)
    grad_inputs = grad_middle + norm_back(
        grad_one, unit_one, inverse_one, first_gain_b.astype(jnp.float32)
    )
    grad_inputs = grad_inputs.astype(jnp.bfloat16).reshape(seqs_here, positions, model_width)
    (
        part_first_gain,
        part_first_shift,
        part_w_query,
        part_b_query,
        part_w_key,
        part_w_value,
        part_b_value,
        part_w_out,
        part_b_out,
        part_second_gain,
        part_second_shift,
        part_w_up,
        part_b_up,
        part_w_down,
        part_b_down,
    ) = (
        lax.psum_scatter(d_first_gain, "dp", scatter_dimension=0, tiled=True),
        lax.psum_scatter(d_first_shift, "dp", scatter_dimension=0, tiled=True),
        lax.psum_scatter(d_w_query, "dp", scatter_dimension=0, tiled=True),
        lax.psum_scatter(d_b_query, "dp", scatter_dimension=0, tiled=True),
        lax.psum_scatter(d_w_key, "dp", scatter_dimension=0, tiled=True),
        lax.psum_scatter(d_w_value, "dp", scatter_dimension=0, tiled=True),
        lax.psum_scatter(d_b_value, "dp", scatter_dimension=0, tiled=True),
        lax.psum_scatter(d_w_out, "dp", scatter_dimension=0, tiled=True),
        lax.psum_scatter(d_b_out, "dp", scatter_dimension=0, tiled=True),
        lax.psum_scatter(d_second_gain, "dp", scatter_dimension=0, tiled=True),
        lax.psum_scatter(d_second_shift, "dp", scatter_dimension=0, tiled=True),
        lax.psum_scatter(d_w_up, "dp", scatter_dimension=0, tiled=True),
        lax.psum_scatter(d_b_up, "dp", scatter_dimension=0, tiled=True),
        lax.psum_scatter(d_w_down, "dp", scatter_dimension=0, tiled=True),
        lax.psum_scatter(d_b_down, "dp", scatter_dimension=0, tiled=True),
    )
    (
        shard_first_gain,
        shard_first_shift,
        shard_w_query,
        shard_b_query,
        shard_w_key,
        shard_w_value,
        shard_b_value,
        shard_w_out,
        shard_b_out,
        shard_second_gain,
        shard_second_shift,
        shard_w_up,
        shard_b_up,
        shard_w_down,
        shard_b_down,
    ) = (
        lax.psum(part_first_gain.astype(jnp.bfloat16), "seq").astype(jnp.float32),
        lax.psum(part_first_shift.astype(jnp.bfloat16), "seq").astype(jnp.float32),
        lax.psum(part_w_query.astype(jnp.bfloat16), "seq").astype(jnp.float32),
        lax.psum(part_b_query.astype(jnp.bfloat16), "seq").astype(jnp.float32),
        lax.psum(part_w_key.astype(jnp.bfloat16), "seq").astype(jnp.float32),
        lax.psum(part_w_value.astype(jnp.bfloat16), "seq").astype(jnp.float32),
        lax.psum(part_b_value.astype(jnp.bfloat16), "seq").astype(jnp.float32),
        lax.psum(part_w_out.astype(jnp.bfloat16), "seq").astype(jnp.float32),
        lax.psum(part_b_out.astype(jnp.bfloat16), "seq").astype(jnp.float32),
        lax.psum(part_second_gain.astype(jnp.bfloat16), "seq").astype(jnp.float32),
        lax.psum(part_second_shift.astype(jnp.bfloat16), "seq").astype(jnp.float32),
        lax.psum(part_w_up.astype(jnp.bfloat16), "seq").astype(jnp.float32),
        lax.psum(part_b_up.astype(jnp.bfloat16), "seq").astype(jnp.float32),
        lax.psum(part_w_down.astype(jnp.bfloat16), "seq").astype(jnp.float32),
        lax.psum(part_b_down.astype(jnp.bfloat16), "seq").astype(jnp.float32),
    )
    return (
        output,
        grad_inputs,
        shard_first_gain,
        shard_first_shift,
        shard_w_query,
        shard_b_query,
        shard_w_key,
        shard_w_value,
        shard_b_value,
        shard_w_out,
        shard_b_out,
        shard_second_gain,
        shard_second_shift,
        shard_w_up,
        shard_b_up,
        shard_w_down,
        shard_b_down,
    )


def solution(mesh):
    placed = (
        P("dp", "seq", None),
        P("dp", "seq"),
        P("dp"),
        P("dp"),
        P("dp", None),
        P("dp"),
        P("dp", None),
        P("dp", None),
        P("dp"),
        P("dp", None),
        P("dp"),
        P("dp"),
        P("dp"),
        P("dp", None),
        P("dp"),
        P("dp", None),
        P("dp"),
        P("dp", "seq", None),
    )
    return jax.shard_map(
        per_device,
        mesh=mesh,
        in_specs=placed,
        out_specs=(
            P("dp", "seq", None),
            P("dp", "seq", None),
            P("dp"),
            P("dp"),
            P("dp", None),
            P("dp"),
            P("dp", None),
            P("dp", None),
            P("dp"),
            P("dp", None),
            P("dp"),
            P("dp"),
            P("dp"),
            P("dp", None),
            P("dp"),
            P("dp", None),
            P("dp"),
        ),
        check_vma=False,
    )
```

profile of v0, /device:TPU:0, one launch (start us, length us, event | category | flops | bytes accessed | tf_op | source)
XLA Modules:
  0.0 1093.1 jit_solution(9284306337476619404)
XLA Ops:
  15.2 26.3 %all-reduce.18 = (bf16[768]{0:T(1024)(128)(2,1)S(1)}, bf16[768]{0:T(1024)(128)(2,1)S(1)}, bf16[768]{0:T(1024)(128)(2,1)S(1)}, bf16[768]{0:T(1024)(128)(2,1)S(1)}...) all-reduce(bf16[768]{0:T(1024)(128)(2,1)S(1)} %dynamic-update-slice, ...), channel_id=1, replica_groups=mesh['dp'=8,'seq'=4] {'dp'}, use_global_device_ids=true, to_apply=%add.1 | all-reduce | flops 6144 | bytes 24576
  47.7 5.0 all-to-all-start
  53.4 9.6 all-gather.12.cloned.1.call-done
  62.9 3.7 add_convert_fusion.2
  66.7 3.6 copy.106
  70.2 16.2 %all-to-all-done = bf16[3,256,768]{1,0,2:T(4,128)(2,1)S(1)} async-done(((bf16[3,256,768]{1,0,2:T(4,128)(2,1)}), bf16[3,256,768]{1,0,2:T(4,128)(2,1)S(1)}, u32[]{:S(2)}, u32[]{:S(2)}) %all-to-all-start) | async-done | bytes 1179680 | tf_op jit(solution)/shard_map/all_to_all | solution.py:170
  86.5 4.3 all-to-all-start.2
  91.4 3.7 convolution_convert_fusion.1
  95.1 3.6 copy.103
  98.7 28.6 %all-to-all-done.2 = bf16[3,256,768]{1,0,2:T(4,128)(2,1)} async-done(((bf16[3,256,768]{1,0,2:T(4,128)(2,1)}), bf16[3,256,768]{1,0,2:T(4,128)(2,1)}, u32[]{:S(2)}, u32[]{:S(2)}) %all-to-all-start.2) | async-done | bytes 1179680 | tf_op jit(solution)/shard_map/all_to_all | solution.py:184
  127.3 4.3 all-to-all-start.1
  132.3 41.2 %all_gather.56 = s32[3,1024]{1,0:T(4,128)S(1)} all-gather(s32[3,256]{1,0:T(4,128)S(1)} %copy-done.26), channel_id=1, replica_groups=mesh['dp'=8,'seq'=4] {'seq'}, dimensions={1}, use_global_device_ids=true | all-gather | bytes 15360 | tf_op jit(solution)/shard_map/all_gather | solution.py:156
  183.2 3.4 reshape.295
  186.6 3.7 copy.111
  197.2 3.7 copy.110
  202.1 99.2 %while.26 = (s32[]{:T(128)}, bf16[9,1024,64]{1,2,0:T(8,128)(2,1)}, f32[9,1024]{1,0:T(8,128)}, s32[9,1024]{1,0:T(8,128)}, bf16[9,1024,64]{2,1,0:T(8,128)(2,1)S(1)...) while((s32[]{:T(128)}, bf16[9,1024,64]{1,2,0:T(8,128)(2,1)}, ...), condition=%wide.region_5.6_spmd, body=%wide.region_2.5_spmd.sunk | while | flops 284228608 | bytes 30349440 | solution.py:197
  208.9 4.2 fusion.156
  219.9 4.2 fusion.156
  231.0 4.2 fusion.156
  242.0 4.2 fusion.156
  253.0 4.2 fusion.156
  264.0 4.2 fusion.156
  275.0 4.2 fusion.156
  286.0 4.2 fusion.156
  297.1 4.2 fusion.156
  301.3 4.2 copy.112
  305.5 4.6 all-to-all-start.3
  311.4 10.1 all-gather
  322.1 33.6 %all-to-all-done.3 = bf16[3,1024,192]{2,0,1:T(4,128)(2,1)} async-done(((bf16[3,1024,192]{2,0,1:T(4,128)(2,1)}), bf16[3,1024,192]{2,0,1:T(4,128)(2,1)}, u32[]{:S(2)}, u32[]{:S(2)}) %all-to-all-start.3) | async-done | bytes 1179680 | tf_op jit(solution)/shard_map/all_to_all | solution.py:201
  364.3 27.2 %fusion.56 = (bf16[768,3072]{1,0:T(8,128)(2,1)}, f32[768,3072]{1,0:T(8,128)}) fusion(f32[3072]{0:T(1024)} %bitcast.275, bf16[768,3072]{1,0:T(8,128)(2,1)} %all-gather.16.cloned.1.call-done, f32[768,768]{1,0:T(8,128)S(1)} %get-tuple-element.265, f32[768]{0:T(1024)S(1)} %convert_element_type.227, f32[768]{0:T(1024)S(1)} %convert_element_type.226, ...), kind=kOutput, calls=%fused_computation.64 | convolution fusion | flops 3782541312 | bytes 21258240 | tf_op jit(solution)/shard_map/dot_general | solution.py:213
  391.5 11.6 %convert_reduce_fusion = (f32[3072]{0:T(1024)}, bf16[768,3072]{1,0:T(8,128)(2,1)S(1)}) fusion(f32[768,3072]{1,0:T(8,128)} %get-tuple-element.267, f32[3072]{0:T(1024)} %bitcast.276, bf16[768,768]{1,0:T(8,128)(2,1)} %bitcast.249, bf16[3072,768]{1,0:T(8,128)(2,1)} %all-gather.18.cloned.1.call-done), kind=kOutput, calls=%fused_computation.71 | convolution fusion | flops 3654546432 | bytes 20078592 | tf_op jit(solution)/shard_map/dot_general | solution.py:40
  403.2 4.8 multiply_reduce_fusion.1
  411.8 3.6 copy.115
  415.4 4.3 all-to-all-start.4
  419.8 4.5 fusion.90
  424.4 31.9 %all-to-all-done.4 = bf16[3,256,768]{1,0,2:T(4,128)(2,1)} async-done(((bf16[3,256,768]{1,0,2:T(4,128)(2,1)}), bf16[3,256,768]{1,0,2:T(4,128)(2,1)}, u32[]{:S(2)}, u32[]{:S(2)}) %all-to-all-start.4) | async-done | bytes 1179680 | tf_op jit(solution)/shard_map/all_to_all | solution.py:252
  459.8 3.8 reshape.303
  467.1 124.2 %while.27 = (s32[]{:T(128)}, bf16[9,1024,64]{1,2,0:T(8,128)(2,1)}, bf16[9,1024,64]{1,2,0:T(8,128)(2,1)}, bf16[9,1024,64]{1,2,0:T(8,128)(2,1)}, s32[9,1024]{1,0:T...) while((s32[]{:T(128)}, bf16[9,1024,64]{1,2,0:T(8,128)(2,1)}, ...), condition=%wide.region_12.13_spmd, body=%wide.region_10.12_spmd.sunk | while | flops 681901056 | bytes 33465460 | solution.py:253
  591.2 4.1 copy.122
  595.3 4.4 all-to-all-start.5
  602.0 45.4 %all-to-all-done.5 = bf16[3,1024,192]{2,0,1:T(4,128)(2,1)} async-done(((bf16[3,1024,192]{2,0,1:T(4,128)(2,1)}), bf16[3,1024,192]{2,0,1:T(4,128)(2,1)}, u32[]{:S(2)}, u32[]{:S(2)}) %all-to-all-start.5) | async-done | bytes 1179680 | tf_op jit(solution)/shard_map/all_to_all | solution.py:265
  647.5 4.2 copy.124
  651.7 4.0 reshape.307
  655.7 4.2 fusion.99
  660.0 4.1 copy.125
  664.0 51.4 %all_to_all.120 = bf16[3,1024,192]{2,0,1:T(4,128)(2,1)S(1)} all-to-all(bf16[3,1024,192]{2,0,1:T(4,128)(2,1)} %copy.125), channel_id=1, replica_groups=mesh['dp'=8,'seq'=4] {'seq'}, dimensions={1} | all-to-all | bytes 2359296 | tf_op jit(solution)/shard_map/all_to_all | solution.py:272
  718.1 4.0 reshape.310
  722.1 4.2 fusion.100
  726.4 4.1 copy.128
  730.5 50.8 %all_to_all.121 = bf16[3,1024,192]{2,0,1:T(4,128)(2,1)S(1)} all-to-all(bf16[3,1024,192]{2,0,1:T(4,128)(2,1)} %copy.128), channel_id=1, replica_groups=mesh['dp'=8,'seq'=4] {'seq'}, dimensions={1} | all-to-all | bytes 2359296 | tf_op jit(solution)/shard_map/all_to_all | solution.py:279
  785.3 4.0 reshape.313
  789.3 4.1 fusion.101
  793.5 9.0 fusion.93
  802.6 10.6 fusion.102
  817.2 8.6 add_convert_fusion
  825.8 4.4 copy.135
  839.9 4.1 fusion.97
  849.0 67.9 %reduce-scatter.15.cloned.1.call-done = f32[96,3072]{1,0:T(8,128)} async-done(((f32[768,3072]{1,0:T(8,128)}), f32[96,3072]{1,0:T(8,128)}) %reduce-scatter.15.cloned.1.call-update) | async-done | bytes 1179664 | tf_op jit(solution)/shard_map/reduce_scatter | solution.py:334
  919.0 77.7 %reduce-scatter.17.cloned.1.call-done = f32[384,768]{1,0:T(8,128)} async-done(((f32[3072,768]{1,0:T(8,128)}), f32[384,768]{1,0:T(8,128)}) %reduce-scatter.17.cloned.1.call-update) | async-done | bytes 1179664 | tf_op jit(solution)/shard_map/reduce_scatter | solution.py:336
  1001.3 3.8 fusion.88
  1005.2 26.3 %all-reduce.17 = (bf16[768]{0:T(1024)(128)(2,1)}, bf16[768]{0:T(1024)(128)(2,1)}, bf16[768]{0:T(1024)(128)(2,1)}, bf16[768]{0:T(1024)(128)(2,1)}, bf16[768]{0:T(...) all-reduce(f32[768]{0:T(1024)} %get-tuple-element.184, ...), channel_id=2, replica_groups=mesh['dp'=8,'seq'=4] {'dp'}, use_global_device_ids=true, to_apply=%region_16.17.clone | all-reduce | flops 9216 | bytes 55296
  1042.2 13.1 %all-reduce.19 = (bf16[96]{0:T(256)(128)(2,1)}, bf16[96]{0:T(256)(128)(2,1)}, bf16[96]{0:T(256)(128)(2,1)}, bf16[96]{0:T(256)(128)(2,1)}, bf16[96]{0:T(256)(128)...) all-reduce(bf16[96]{0:T(256)(128)(2,1)} %dynamic-slice.43, ...), channel_id=1, replica_groups=mesh['dp'=8,'seq'=4] {'seq'}, use_global_device_ids=true, to_apply=%region_17.18 | all-reduce | flops 1152 | bytes 4608 | tf_op jit(solution)/shard_map/psum | solution.py:356
  1067.3 3.5 fusion.87
  1070.8 8.2 all-reduce.23.cloned.1.call-done
  (366 shorter events, 302.6 us)
Async XLA Ops:
  7.2 4.9 copy-start.31
  7.2 34.9 %copy-start.1 = (bf16[3,256,768]{2,1,0:T(8,128)(2,1)S(1)}, bf16[3,256,768]{2,1,0:T(8,128)(2,1)}, u32[]{:S(2)}) copy-start(bf16[3,256,768]{2,1,0:T(8,128)(2,1)} %param.22) | copy-start | bytes 3538948
  7.2 6.1 copy-start.36
  7.2 6.4 copy-start.37
  7.2 6.6 copy-start.38
  7.2 6.8 copy-start.39
  7.3 7.0 copy-start.40
  7.3 7.3 copy-start.41
  7.3 7.5 copy-start.42
  7.3 7.7 copy-start.43
  7.3 35.4 %all-gather.8.cloned.1.call-start = ((), (), s32[]{:S(2)}) async-start(), calls=%async_computation.14 | async-start | bytes 1327104 | tf_op jit(solution)/shard_map/all_gather | solution.py:142
  8.0 54.9 %all-gather.12.cloned.1.call-start = ((), (), s32[]{:S(2)}) async-start(), calls=%async_computation.16 | async-start | bytes 1327104 | tf_op jit(solution)/shard_map/all_gather | solution.py:145
  10.3 31.3 %copy-start.18 = (f32[3,256]{1,0:T(4,128)}, f32[3,256]{1,0:T(4,128)S(1)}, u32[]{:S(2)}) copy-start(f32[3,256]{1,0:T(4,128)S(1)} %broadcast_multiply_fusion.5) | copy-start | bytes 9220
  12.1 30.6 %copy-start.19 = (f32[768]{0:T(1024)}, f32[768]{0:T(1024)S(1)}, u32[]{:S(2)}) copy-start(f32[768]{0:T(1024)S(1)} %div.35) | copy-start | bytes 9220
  42.7 2.8 copy-start.9
  47.7 38.8 %all-to-all-start = ((bf16[3,256,768]{1,0,2:T(4,128)(2,1)}), bf16[3,256,768]{1,0,2:T(4,128)(2,1)S(1)}, u32[]{:S(2)}, u32[]{:S(2)}) async-start(bf16[3,256,768]{1,0,2:T(4,128)(2,1)} %copy.100), calls=%async_computation | async-start | bytes 3145728 | tf_op jit(solution)/shard_map/all_to_all | solution.py:170
  52.6 38.8 %all-gather.10.cloned.1.call-start = ((), (), s32[]{:S(2)}) async-start(), calls=%async_computation.15 | async-start | bytes 1327104 | tf_op jit(solution)/shard_map/all_gather | solution.py:144
  86.5 40.9 %all-to-all-start.2 = ((bf16[3,256,768]{1,0,2:T(4,128)(2,1)}), bf16[3,256,768]{1,0,2:T(4,128)(2,1)}, u32[]{:S(2)}, u32[]{:S(2)}) async-start(bf16[3,256,768]{1,0,2:T(4,128)(2,1)} %copy.106), calls=%async_computation.2 | async-start | bytes 3145728 | tf_op jit(solution)/shard_map/all_to_all | solution.py:184
  90.8 270.2 %all-gather.14.cloned.1.call-start = ((), (), s32[]{:S(2)}) async-start(), calls=%async_computation.17 | async-start | bytes 1327104 | tf_op jit(solution)/shard_map/all_gather | solution.py:147
  98.7 33.6 %copy-start.26 = (s32[3,256]{1,0:T(4,128)S(1)}, s32[3,256]{1,0:T(4,128)}, u32[]{:S(2)}) copy-start(s32[3,256]{1,0:T(4,128)} %param.23) | copy-start | bytes 9220
  127.3 63.0 %all-to-all-start.1 = ((bf16[3,256,768]{1,0,2:T(4,128)(2,1)}), bf16[3,256,768]{1,0,2:T(4,128)(2,1)}, u32[]{:S(2)}, u32[]{:S(2)}) async-start(bf16[3,256,768]{1,0,2:T(4,128)(2,1)} %copy.103), calls=%async_computation.1 | async-start | bytes 3145728 | tf_op jit(solution)/shard_map/all_to_all | solution.py:177
  131.7 232.6 %all-gather.16.cloned.1.call-start = ((), (), s32[]{:S(2)}) async-start(), calls=%async_computation.18 | async-start | bytes 5308416 | tf_op jit(solution)/shard_map/all_gather | solution.py:151
  204.5 1.9 copy-start
  215.5 1.9 copy-start
  226.6 1.9 copy-start
  237.6 1.9 copy-start
  248.6 1.9 copy-start
  259.6 1.9 copy-start
  270.6 1.9 copy-start
  281.7 1.9 copy-start
  292.7 1.9 copy-start
  301.3 4.3 copy-start.4
  305.5 5.2 copy-start.30
  305.5 5.2 copy-start.29
  305.5 5.2 copy-start.28
  305.5 50.2 %all-to-all-start.3 = ((bf16[3,1024,192]{2,0,1:T(4,128)(2,1)}), bf16[3,1024,192]{2,0,1:T(4,128)(2,1)}, u32[]{:S(2)}, u32[]{:S(2)}) async-start(bf16[3,1024,192]{2,0,1:T(4,128)(2,1)} %copy.112), calls=%async_computation.3 | async-start | bytes 4194304 | tf_op jit(solution)/shard_map/all_to_all | solution.py:201
  310.1 81.4 %all-gather.18.cloned.1.call-start = ((), (), s32[]{:S(2)}) async-start(), calls=%async_computation.19 | async-start | bytes 5308416 | tf_op jit(solution)/shard_map/all_gather | solution.py:153
  391.5 11.6 %copy-start.32 = (bf16[768,3072]{1,0:T(8,128)(2,1)S(1)}, bf16[768,3072]{1,0:T(8,128)(2,1)}, u32[]{:S(2)}) copy-start(bf16[768,3072]{1,0:T(8,128)(2,1)} %all-gather.16.cloned.1.call-done) | copy-start | bytes 14155780
  403.2 4.8 copy-start.8
  403.2 4.8 copy-start.7
  408.0 1.7 copy-start.35
  409.7 2.2 copy-start.5
  415.4 40.9 %all-to-all-start.4 = ((bf16[3,256,768]{1,0,2:T(4,128)(2,1)}), bf16[3,256,768]{1,0,2:T(4,128)(2,1)}, u32[]{:S(2)}, u32[]{:S(2)}) async-start(bf16[3,256,768]{1,0,2:T(4,128)(2,1)} %copy.115), calls=%async_computation.4 | async-start | bytes 3145728 | tf_op jit(solution)/shard_map/all_to_all | solution.py:252
  419.8 418.5 %reduce-scatter.13.cloned.1.call-start = ((), (), s32[]{:S(2)}) async-start(), calls=%async_computation.23 | async-start | bytes 2654208 | tf_op jit(solution)/shard_map/reduce_scatter | solution.py:330
  595.3 52.1 %all-to-all-start.5 = ((bf16[3,1024,192]{2,0,1:T(4,128)(2,1)}), bf16[3,1024,192]{2,0,1:T(4,128)(2,1)}, u32[]{:S(2)}, u32[]{:S(2)}) async-start(bf16[3,1024,192]{2,0,1:T(4,128)(2,1)} %copy.122), calls=%async_computation.5 | async-start | bytes 4194304 | tf_op jit(solution)/shard_map/all_to_all | solution.py:265
  599.8 244.3 %reduce-scatter.7.cloned.1.call-start = ((), (), s32[]{:S(2)}) async-start(), calls=%async_computation.20 | async-start | bytes 2654208 | tf_op jit(solution)/shard_map/reduce_scatter | solution.py:325
  659.9 185.7 %reduce-scatter.9.cloned.1.call-start = ((), (), s32[]{:S(2)}) async-start(), calls=%async_computation.21 | async-start | bytes 2654208 | tf_op jit(solution)/shard_map/reduce_scatter | solution.py:327
  726.4 120.9 %reduce-scatter.11.cloned.1.call-start = ((), (), s32[]{:S(2)}) async-start(), calls=%async_computation.22 | async-start | bytes 2654208 | tf_op jit(solution)/shard_map/reduce_scatter | solution.py:328
  781.3 1.4 copy-start.2
  793.5 123.4 %reduce-scatter.15.cloned.1.call-start = ((), (), s32[]{:S(2)}) async-start(), calls=%async_computation.24 | async-start | bytes 10616832 | tf_op jit(solution)/shard_map/reduce_scatter | solution.py:334
  802.5 194.2 %reduce-scatter.17.cloned.1.call-start = ((), (), s32[]{:S(2)}) async-start(), calls=%async_computation.25 | async-start | bytes 10616832 | tf_op jit(solution)/shard_map/reduce_scatter | solution.py:336
  813.2 1.6 copy-start.27
  813.2 265.8 %all-reduce.23.cloned.1.call-start = ((), (), s32[]{:S(2)}) async-start(), calls=%async_computation.26 | async-start | bytes 3538944 | tf_op jit(solution)/shard_map/psum | solution.py:358
  825.8 7.0 copy-start.3
  849.0 149.9 %copy-start.10 = (bf16[768,768]{1,0:T(8,128)(2,1)S(1)}, bf16[768,768]{1,0:T(8,128)(2,1)}, u32[]{:S(2)}) copy-start(bf16[768,768]{1,0:T(8,128)(2,1)} %reshape.310) | copy-start | bytes 3538948
  849.0 149.9 %copy-start.34 = (bf16[768,768]{1,0:T(8,128)(2,1)S(1)}, bf16[768,768]{1,0:T(8,128)(2,1)}, u32[]{:S(2)}) copy-start(bf16[768,768]{1,0:T(8,128)(2,1)} %all-gather.10.cloned.1.call-done) | copy-start | bytes 3538948
  999.0 1.6 copy-start.33
  999.0 2.4 copy-start.44
  1001.3 3.8 copy-start.25
  1001.3 65.9 %copy-start.6 = (f32[768,768]{1,0:T(8,128)S(1)}, f32[768,768]{1,0:T(8,128)}, u32[]{:S(2)}) copy-start(f32[768,768]{1,0:T(8,128)} %copy-done.5) | copy-start | bytes 7077892
  1079.0 4.4 copy-start.15
  1079.0 5.1 copy-start.14
  1079.0 5.9 copy-start.13
  1079.0 6.6 copy-start.12
  (8 other events, 9.0 us)
Sparse Core Ops, SparseCore 0:
  10.0 26.8 all-gather.7
  38.8 24.0 all-gather.11
  64.8 24.0 all-gather.9
  93.2 26.1 all-gather.13
  134.1 41.8 all-gather.15
  312.5 41.8 all-gather.17
  424.5 45.4 reduce-scatter.12
  660.0 43.1 reduce-scatter.6
  726.5 43.1 reduce-scatter.8
  793.6 43.2 reduce-scatter.10
  840.4 76.4 reduce-scatter.14
  920.2 76.4 reduce-scatter.16
  1000.7 78.2 all-reduce.22
where the time goes:
time: 1110 us; the launch traced here: 1090 us
  waiting for transfers between devices  323 us (29%)
  matrix products  266 us (24%)
  blocking collectives  219 us (20%)
  local copies, waits for them, and re-layouts  172 us (15%)
  other arithmetic  68 us (6%)
  starting transfers between devices  27.7 us (2%)
  between operations  16.7 us (2%)
    reduce_scatter x1, waiting for transfers between devices, per_device(): lax.psum_scatter(d_w_down, 'dp', scatter_dimension=0, tiled=True)  77.7 us
    reduce_scatter x1, waiting for transfers between devices, per_device(): lax.psum_scatter(d_w_up, 'dp', scatter_dimension=0, tiled=True)  67.9 us
    unnamed x2, blocking collectives  52.5 us
    all_to_all x1, blocking collectives, per_device(): lax.all_to_all(from_pairs(grad_key_pairs, seqs_here, heads_here), 'seq',...  51.4 us
    all_to_all x1, blocking collectives, per_device(): lax.all_to_all(from_pairs(grad_value_pairs, seqs_here, heads_here), 'seq'...  50.8 us
    all_to_all x1, waiting for transfers between devices, per_device(): lax.all_to_all(from_pairs(grad_query_pairs, seqs_here, heads_here), 'seq'...  45.4 us
    all_gather x1, blocking collectives, per_device(): full_segments = lax.all_gather(segment_ids, 'seq', axis=1, tiled=True)  41.2 us
    dot_general x18, matrix products, masked_scores(): jnp.einsum('qd,kd->qk', query_pair, key_pair, preferred_element_type=jnp....  38.3 us
  transfers between devices with their start and end apart: 19, of which 9 were waited for; matrix products, arithmetic and copies ran while one was open for 41% of the time, Pallas kernels for 0%

commit v1 on v0

--- a/solution.py
+++ b/solution.py
@@ -1,3 +1,4 @@
+import functools
 import jax
 import jax.numpy as jnp
 from jax import lax
@@ -5,6 +6,40 @@
 
 HD = 64
 EPSILON = 1e-05
+
+
+def touch_edge(u_in, k_dim, matrix):
+    current_arr = u_in.shape
+    base_arr = u_in.reshape(
+        *current_arr[:k_dim], matrix, current_arr[k_dim] // matrix, *current_arr[k_dim + 1 :]
+    )
+    return jnp.moveaxis(base_arr, k_dim, 0)
+
+
+def surface_match(t0, axis_k):
+    part_next = list(t0.shape[1:])
+    part_next[axis_k] *= t0.shape[0]
+    return jnp.moveaxis(t0, 0, axis_k).reshape(part_next)
+
+
+def types_compute(x_in, peer_axis, z, m):
+    z1 = lax.axis_size(peer_axis)
+    now = lax.axis_index(peer_axis)
+    v_now, outcome_arr = (z1, now)
+    block_out = touch_edge(x_in, z, v_now)
+    buffer = [block_out[outcome_arr]]
+    for src_i in range(1, v_now):
+        g_now = block_out[outcome_arr ^ src_i]
+        reached = lax.ppermute(
+            g_now, axis_name=peer_axis, perm=[(b, b ^ src_i) for b in range(v_now)]
+        )
+        buffer.append(reached)
+    current_block = jnp.stack(buffer, 0)
+    block_out = current_block[outcome_arr ^ jnp.arange(v_now)]
+    return surface_match(block_out, m)
+
+
+record_match = functools.partial(types_compute, peer_axis="seq", z=2, m=1)
 
 
 def layer_norm(values, gain, shift):
@@ -167,13 +202,7 @@
         jnp.dot(act_one, w_value, preferred_element_type=jnp.float32) + b_value.astype(jnp.float32)
     ).astype(jnp.bfloat16)
     query_heads, key_heads, value_heads = (
-        lax.all_to_all(
-            query_tok.reshape(seqs_here, positions, model_width),
-            "seq",
-            split_axis=2,
-            concat_axis=1,
-            tiled=True,
-        ),
+        record_match(query_tok.reshape(seqs_here, positions, model_width)),
         lax.all_to_all(
             key_tok.reshape(seqs_here, positions, model_width),
             "seq",

time: 1110 us -> 1100 us (level)
  waiting for transfers between devices: 323 us -> 295 us
  local copies, waits for them, and re-layouts: 172 us -> 191 us
    another operation x4 -> x11, local copies, waits for them, and re-layouts: 4.63 us -> 22.2 us
    all_to_all x1 -> x0, waiting for transfers between devices: 16.2 us -> none  [per_device(): lax.all_to_all(query_tok.reshape(seqs_here, positions, model_width), 'seq...]
    unnamed x115 -> x105, local copies, waits for them, and re-layouts: 17.2 us -> 23.6 us
  transfers between devices with their start and end apart: 19 -> 21, of which waited for: 9 -> 8; matrix products, arithmetic and copies ran while one was open for 41% -> 43% of each run, Pallas kernels for 0% -> 0%
where the time goes in v1:
time: 1100 us; the launch traced here: 1090 us
  waiting for transfers between devices  295 us (27%)
  matrix products  266 us (24%)
  blocking collectives  221 us (20%)
  local copies, waits for them, and re-layouts  191 us (17%)
  other arithmetic  67.8 us (6%)
  starting transfers between devices  27.7 us (3%)
  between operations  16.7 us (2%)
    reduce_scatter x1, waiting for transfers between devices, per_device(): lax.psum_scatter(d_w_down, 'dp', scatter_dimension=0, tiled=True)  77.7 us
    reduce_scatter x1, waiting for transfers between devices, per_device(): lax.psum_scatter(d_w_up, 'dp', scatter_dimension=0, tiled=True)  68.6 us
    unnamed x2, blocking collectives  52.5 us
    all_to_all x1, blocking collectives, per_device(): lax.all_to_all(from_pairs(grad_key_pairs, seqs_here, heads_here), 'seq',...  51.5 us
    all_to_all x1, blocking collectives, per_device(): lax.all_to_all(from_pairs(grad_value_pairs, seqs_here, heads_here), 'seq'...  50.8 us
    all_to_all x1, waiting for transfers between devices, per_device(): lax.all_to_all(from_pairs(grad_query_pairs, seqs_here, heads_here), 'seq'...  45.5 us
    all_gather x1, blocking collectives, per_device(): full_segments = lax.all_gather(segment_ids, 'seq', axis=1, tiled=True)  43.3 us
    dot_general x18, matrix products, masked_scores(): jnp.einsum('qd,kd->qk', query_pair, key_pair, preferred_element_type=jnp....  38.3 us
  transfers between devices with their start and end apart: 21, of which 8 were waited for; matrix products, arithmetic and copies ran while one was open for 43% of the time, Pallas kernels for 0%

profile of v1, /device:TPU:0, one launch (start us, length us, event | category | flops | bytes accessed | tf_op | source)
XLA Modules:
  0.0 1086.0 jit_solution(10602582125430366314)
XLA Ops:
  18.1 26.2 %all-reduce.18 = (bf16[768]{0:T(1024)(128)(2,1)S(1)}, bf16[768]{0:T(1024)(128)(2,1)S(1)}, bf16[768]{0:T(1024)(128)(2,1)S(1)}, bf16[768]{0:T(1024)(128)(2,1)S(1)}...) all-reduce(bf16[768]{0:T(1024)(128)(2,1)S(1)} %dynamic-update-slice, ...), channel_id=1, replica_groups=mesh['dp'=8,'seq'=4] {'dp'}, use_global_device_ids=true, to_apply=%add.1 | all-reduce | flops 6144 | bytes 24576
  52.6 4.9 all-to-all-start.1
  58.0 4.8 all-gather.10.cloned.1.call-done
  62.8 3.7 convolution_convert_fusion.1
  66.5 3.6 copy.113
  70.1 21.2 %all-to-all-done.1 = bf16[3,256,768]{1,0,2:T(4,128)(2,1)S(1)} async-done(((bf16[3,256,768]{1,0,2:T(4,128)(2,1)}), bf16[3,256,768]{1,0,2:T(4,128)(2,1)S(1)}, u32[]{:S(2)}, u32[]{:S(2)}) %all-to-all-start.1) | async-done | bytes 1179680 | tf_op jit(solution)/shard_map/all_to_all | solution.py:213
  91.3 4.4 all-to-all-start
  95.8 3.8 add_convert_fusion.3
  99.5 3.5 reshape_reshape.6
  103.0 4.6 constant_dynamic-slice_fusion.6
  119.4 43.3 %all_gather.56 = s32[3,1024]{1,0:T(4,128)S(1)} all-gather(s32[3,256]{1,0:T(4,128)S(1)} %copy-done.30), channel_id=1, replica_groups=mesh['dp'=8,'seq'=4] {'seq'}, dimensions={1}, use_global_device_ids=true | all-gather | bytes 15360 | tf_op jit(solution)/shard_map/all_gather | solution.py:191
  175.5 3.4 reshape.309
  178.9 3.7 copy.121
  186.2 3.4 reshape.306
  189.5 3.7 copy.120
  194.4 99.3 %while.26 = (s32[]{:T(128)}, bf16[9,1024,64]{1,2,0:T(8,128)(2,1)}, f32[9,1024]{1,0:T(8,128)}, s32[9,1024]{1,0:T(8,128)}, bf16[9,1024,64]{2,1,0:T(8,128)(2,1)S(1)...) while((s32[]{:T(128)}, bf16[9,1024,64]{1,2,0:T(8,128)(2,1)}, ...), condition=%wide.region_5.6_spmd, body=%wide.region_2.5_spmd.sunk | while | flops 284228608 | bytes 30349440 | solution.py:226
  201.3 4.2 fusion.157
  212.3 4.2 fusion.157
  223.3 4.2 fusion.157
  234.4 4.2 fusion.157
  245.4 4.2 fusion.157
  256.4 4.2 fusion.157
  267.5 4.2 fusion.157
  278.5 4.2 fusion.157
  289.5 4.2 fusion.157
  293.7 4.3 copy.122
  298.0 4.6 all-to-all-start.2
  303.9 10.0 all-gather
  314.5 33.5 %all-to-all-done.2 = bf16[3,1024,192]{2,0,1:T(4,128)(2,1)} async-done(((bf16[3,1024,192]{2,0,1:T(4,128)(2,1)}), bf16[3,1024,192]{2,0,1:T(4,128)(2,1)}, u32[]{:S(2)}, u32[]{:S(2)}) %all-to-all-start.2) | async-done | bytes 1179680 | tf_op jit(solution)/shard_map/all_to_all | solution.py:230
  356.6 27.3 %fusion.56 = (bf16[768,3072]{1,0:T(8,128)(2,1)}, f32[768,3072]{1,0:T(8,128)}) fusion(f32[3072]{0:T(1024)} %bitcast.283, bf16[768,3072]{1,0:T(8,128)(2,1)} %all-gather.16.cloned.1.call-done, f32[768,768]{1,0:T(8,128)S(1)} %get-tuple-element.269, f32[768]{0:T(1024)S(1)} %convert_element_type.227, f32[768]{0:T(1024)S(1)} %convert_element_type.226, ...), kind=kOutput, calls=%fused_computation.65 | convolution fusion | flops 3782541312 | bytes 21258240 | tf_op jit(solution)/shard_map/dot_general | solution.py:242
  383.9 11.6 %convert_reduce_fusion = (f32[3072]{0:T(1024)}, bf16[768,3072]{1,0:T(8,128)(2,1)S(1)}) fusion(f32[768,3072]{1,0:T(8,128)} %get-tuple-element.271, f32[3072]{0:T(1024)} %bitcast.284, bf16[768,768]{1,0:T(8,128)(2,1)} %bitcast.256, bf16[3072,768]{1,0:T(8,128)(2,1)} %all-gather.18.cloned.1.call-done), kind=kOutput, calls=%fused_computation.72 | convolution fusion | flops 3654546432 | bytes 20078592 | tf_op jit(solution)/shard_map/dot_general | solution.py:75
  395.5 4.8 multiply_reduce_fusion.1
  404.2 3.6 copy.125
  407.8 4.3 all-to-all-start.3
  412.2 4.5 fusion.91
  416.8 31.9 %all-to-all-done.3 = bf16[3,256,768]{1,0,2:T(4,128)(2,1)} async-done(((bf16[3,256,768]{1,0,2:T(4,128)(2,1)}), bf16[3,256,768]{1,0,2:T(4,128)(2,1)}, u32[]{:S(2)}, u32[]{:S(2)}) %all-to-all-start.3) | async-done | bytes 1179680 | tf_op jit(solution)/shard_map/all_to_all | solution.py:281
  452.2 3.8 reshape.317
  459.4 124.2 %while.27 = (s32[]{:T(128)}, bf16[9,1024,64]{1,2,0:T(8,128)(2,1)}, bf16[9,1024,64]{1,2,0:T(8,128)(2,1)}, bf16[9,1024,64]{1,2,0:T(8,128)(2,1)}, s32[9,1024]{1,0:T...) while((s32[]{:T(128)}, bf16[9,1024,64]{1,2,0:T(8,128)(2,1)}, ...), condition=%wide.region_12.13_spmd, body=%wide.region_10.12_spmd.sunk | while | flops 681901056 | bytes 33465460 | solution.py:282
  583.6 4.1 copy.132
  587.7 4.5 all-to-all-start.4
  594.4 45.5 %all-to-all-done.4 = bf16[3,1024,192]{2,0,1:T(4,128)(2,1)} async-done(((bf16[3,1024,192]{2,0,1:T(4,128)(2,1)}), bf16[3,1024,192]{2,0,1:T(4,128)(2,1)}, u32[]{:S(2)}, u32[]{:S(2)}) %all-to-all-start.4) | async-done | bytes 1179680 | tf_op jit(solution)/shard_map/all_to_all | solution.py:294
  639.9 4.2 copy.134
  644.1 4.0 reshape.321
  648.1 4.2 fusion.100
  652.3 4.1 copy.135
  656.4 51.5 %all_to_all.105 = bf16[3,1024,192]{2,0,1:T(4,128)(2,1)S(1)} all-to-all(bf16[3,1024,192]{2,0,1:T(4,128)(2,1)} %copy.135), channel_id=1, replica_groups=mesh['dp'=8,'seq'=4] {'seq'}, dimensions={1} | all-to-all | bytes 2359296 | tf_op jit(solution)/shard_map/all_to_all | solution.py:301
  710.6 4.0 reshape.324
  714.6 4.2 fusion.101
  718.9 4.1 copy.138
  722.9 50.8 %all_to_all.106 = bf16[3,1024,192]{2,0,1:T(4,128)(2,1)S(1)} all-to-all(bf16[3,1024,192]{2,0,1:T(4,128)(2,1)} %copy.138), channel_id=1, replica_groups=mesh['dp'=8,'seq'=4] {'seq'}, dimensions={1} | all-to-all | bytes 2359296 | tf_op jit(solution)/shard_map/all_to_all | solution.py:308
  777.7 4.0 reshape.327
  781.7 4.1 fusion.102
  785.9 9.0 fusion.94
  795.0 10.6 fusion.103
  809.3 8.6 add_convert_fusion
  817.9 4.4 copy.145
  832.0 4.1 fusion.98
  841.1 68.6 %reduce-scatter.15.cloned.1.call-done = f32[96,3072]{1,0:T(8,128)} async-done(((f32[768,3072]{1,0:T(8,128)}), f32[96,3072]{1,0:T(8,128)}) %reduce-scatter.15.cloned.1.call-update) | async-done | bytes 1179664 | tf_op jit(solution)/shard_map/reduce_scatter | solution.py:363
  912.0 77.7 %reduce-scatter.17.cloned.1.call-done = f32[384,768]{1,0:T(8,128)} async-done(((f32[3072,768]{1,0:T(8,128)}), f32[384,768]{1,0:T(8,128)}) %reduce-scatter.17.cloned.1.call-update) | async-done | bytes 1179664 | tf_op jit(solution)/shard_map/reduce_scatter | solution.py:365
  994.3 3.8 fusion.88
  998.1 26.3 %all-reduce.17 = (bf16[768]{0:T(1024)(128)(2,1)}, bf16[768]{0:T(1024)(128)(2,1)}, bf16[768]{0:T(1024)(128)(2,1)}, bf16[768]{0:T(1024)(128)(2,1)}, bf16[768]{0:T(...) all-reduce(f32[768]{0:T(1024)} %get-tuple-element.184, ...), channel_id=2, replica_groups=mesh['dp'=8,'seq'=4] {'dp'}, use_global_device_ids=true, to_apply=%region_16.17.clone | all-reduce | flops 9216 | bytes 55296
  1035.2 13.1 %all-reduce.19 = (bf16[96]{0:T(256)(128)(2,1)}, bf16[96]{0:T(256)(128)(2,1)}, bf16[96]{0:T(256)(128)(2,1)}, bf16[96]{0:T(256)(128)(2,1)}, bf16[96]{0:T(256)(128)...) all-reduce(bf16[96]{0:T(256)(128)(2,1)} %dynamic-slice.63, ...), channel_id=1, replica_groups=mesh['dp'=8,'seq'=4] {'seq'}, use_global_device_ids=true, to_apply=%region_17.18 | all-reduce | flops 1152 | bytes 4608 | tf_op jit(solution)/shard_map/psum | solution.py:385
  1060.2 3.5 fusion.87
  1063.7 8.2 all-reduce.23.cloned.1.call-done
  (368 shorter events, 317.6 us)
Async XLA Ops:
  7.2 38.7 %copy-start.1 = (bf16[3,256,768]{2,1,0:T(8,128)(2,1)S(1)}, bf16[3,256,768]{2,1,0:T(8,128)(2,1)}, u32[]{:S(2)}) copy-start(bf16[3,256,768]{2,1,0:T(8,128)(2,1)} %param.22) | copy-start | bytes 3538948
  7.2 40.4 %all-gather.12.cloned.1.call-start = ((), (), s32[]{:S(2)}) async-start(), calls=%async_computation.15 | async-start | bytes 1327104 | tf_op jit(solution)/shard_map/all_gather | solution.py:180
  7.9 54.9 %all-gather.10.cloned.1.call-start = ((), (), s32[]{:S(2)}) async-start(), calls=%async_computation.14 | async-start | bytes 1327104 | tf_op jit(solution)/shard_map/all_gather | solution.py:179
  8.7 87.1 %all-gather.8.cloned.1.call-start = ((), (), s32[]{:S(2)}) async-start(), calls=%async_computation.13 | async-start | bytes 1327104 | tf_op jit(solution)/shard_map/all_gather | solution.py:177
  44.3 3.2 copy-start.20
  44.3 3.2 copy-start.27
  45.9 1.6 copy-start.23
  47.5 2.8 copy-start.11
  52.6 38.7 %all-to-all-start.1 = ((bf16[3,256,768]{1,0,2:T(4,128)(2,1)}), bf16[3,256,768]{1,0,2:T(4,128)(2,1)S(1)}, u32[]{:S(2)}, u32[]{:S(2)}) async-start(bf16[3,256,768]{1,0,2:T(4,128)(2,1)} %copy.116), calls=%async_computation.1 | async-start | bytes 3145728 | tf_op jit(solution)/shard_map/all_to_all | solution.py:213
  57.4 295.9 %all-gather.14.cloned.1.call-start = ((), (), s32[]{:S(2)}) async-start(), calls=%async_computation.16 | async-start | bytes 1327104 | tf_op jit(solution)/shard_map/all_gather | solution.py:182
  91.3 4.5 copy-start.7
  91.3 91.4 %all-to-all-start = ((bf16[3,256,768]{1,0,2:T(4,128)(2,1)}), bf16[3,256,768]{1,0,2:T(4,128)(2,1)}, u32[]{:S(2)}, u32[]{:S(2)}) async-start(bf16[3,256,768]{1,0,2:T(4,128)(2,1)} %copy.113), calls=%async_computation | async-start | bytes 3145728 | tf_op jit(solution)/shard_map/all_to_all | solution.py:206
  95.6 261.0 %all-gather.16.cloned.1.call-start = ((), (), s32[]{:S(2)}) async-start(), calls=%async_computation.17 | async-start | bytes 5308416 | tf_op jit(solution)/shard_map/all_gather | solution.py:186
  107.6 10.0 copy-start.10
  107.6 11.8 %copy-start.30 = (s32[3,256]{1,0:T(4,128)S(1)}, s32[3,256]{1,0:T(4,128)}, u32[]{:S(2)}) copy-start(s32[3,256]{1,0:T(4,128)} %param.23) | copy-start | bytes 9220
  110.5 53.4 %collective-permute-start = (bf16[3,256,192]{1,2,0:T(8,128)(2,1)}, bf16[3,256,192]{1,2,0:T(8,128)(2,1)S(1)}, u32[]{:S(2)}, u32[]{:S(2)}) collective-permute-start(bf16[3,256,192]{1,2,0:T(8,128)(2,1)} %bitcast.18), channel_id=1, source_target_pairs={{0,1},{1,0},{2,3},{3,2},{4,5},{5,4},{6,7},{7,6},{8,9},{9,8},{10,11... | collective-permute-start | bytes 884744 | tf_op jit(solution)/shard_map/ppermute | solution.py:33
  115.2 48.7 %collective-permute-start.1 = (bf16[3,256,192]{1,2,0:T(8,128)(2,1)}, bf16[3,256,192]{1,2,0:T(8,128)(2,1)}, u32[]{:S(2)}, u32[]{:S(2)}) collective-permute-start(bf16[3,256,192]{1,2,0:T(8,128)(2,1)} %bitcast.20), channel_id=1, source_target_pairs={{0,2},{1,3},{2,0},{3,1},{4,6},{5,7},{6,4},{7,5},{8,10},{9,11},{10,... | collective-permute-start | bytes 884744 | tf_op jit(solution)/shard_map/ppermute | solution.py:33
  119.2 44.8 %collective-permute-start.2 = (bf16[3,256,192]{1,2,0:T(8,128)(2,1)}, bf16[3,256,192]{1,2,0:T(8,128)(2,1)S(1)}, u32[]{:S(2)}, u32[]{:S(2)}) collective-permute-start(bf16[3,256,192]{1,2,0:T(8,128)(2,1)} %bitcast.22), channel_id=1, source_target_pairs={{0,3},{1,2},{2,1},{3,0},{4,7},{5,6},{6,5},{7,4},{8,11},{9,10},{10,... | collective-permute-start | bytes 884744 | tf_op jit(solution)/shard_map/ppermute | solution.py:33
  196.9 1.9 copy-start
  207.9 1.9 copy-start
  218.9 1.9 copy-start
  230.0 1.9 copy-start
  241.0 1.9 copy-start
  252.0 1.9 copy-start
  263.1 1.9 copy-start
  274.1 1.9 copy-start
  285.1 1.9 copy-start
  293.7 4.3 copy-start.4
  298.0 5.2 copy-start.34
  298.0 5.2 copy-start.33
  298.0 5.2 copy-start.32
  298.0 50.0 %all-to-all-start.2 = ((bf16[3,1024,192]{2,0,1:T(4,128)(2,1)}), bf16[3,1024,192]{2,0,1:T(4,128)(2,1)}, u32[]{:S(2)}, u32[]{:S(2)}) async-start(bf16[3,1024,192]{2,0,1:T(4,128)(2,1)} %copy.122), calls=%async_computation.2 | async-start | bytes 4194304 | tf_op jit(solution)/shard_map/all_to_all | solution.py:230
  302.6 81.3 %all-gather.18.cloned.1.call-start = ((), (), s32[]{:S(2)}) async-start(), calls=%async_computation.18 | async-start | bytes 5308416 | tf_op jit(solution)/shard_map/all_gather | solution.py:188
  383.9 11.6 %copy-start.35 = (bf16[768,3072]{1,0:T(8,128)(2,1)S(1)}, bf16[768,3072]{1,0:T(8,128)(2,1)}, u32[]{:S(2)}) copy-start(bf16[768,3072]{1,0:T(8,128)(2,1)} %all-gather.16.cloned.1.call-done) | copy-start | bytes 14155780
  395.5 4.8 copy-start.9
  395.5 4.8 copy-start.8
  400.4 1.7 copy-start.38
  402.1 2.2 copy-start.5
  407.8 40.9 %all-to-all-start.3 = ((bf16[3,256,768]{1,0,2:T(4,128)(2,1)}), bf16[3,256,768]{1,0,2:T(4,128)(2,1)}, u32[]{:S(2)}, u32[]{:S(2)}) async-start(bf16[3,256,768]{1,0,2:T(4,128)(2,1)} %copy.125), calls=%async_computation.3 | async-start | bytes 3145728 | tf_op jit(solution)/shard_map/all_to_all | solution.py:281
  412.1 418.2 %reduce-scatter.13.cloned.1.call-start = ((), (), s32[]{:S(2)}) async-start(), calls=%async_computation.22 | async-start | bytes 2654208 | tf_op jit(solution)/shard_map/reduce_scatter | solution.py:359
  587.7 52.2 %all-to-all-start.4 = ((bf16[3,1024,192]{2,0,1:T(4,128)(2,1)}), bf16[3,1024,192]{2,0,1:T(4,128)(2,1)}, u32[]{:S(2)}, u32[]{:S(2)}) async-start(bf16[3,1024,192]{2,0,1:T(4,128)(2,1)} %copy.132), calls=%async_computation.4 | async-start | bytes 4194304 | tf_op jit(solution)/shard_map/all_to_all | solution.py:294
  592.1 244.0 %reduce-scatter.7.cloned.1.call-start = ((), (), s32[]{:S(2)}) async-start(), calls=%async_computation.19 | async-start | bytes 2654208 | tf_op jit(solution)/shard_map/reduce_scatter | solution.py:354
  652.3 185.5 %reduce-scatter.9.cloned.1.call-start = ((), (), s32[]{:S(2)}) async-start(), calls=%async_computation.20 | async-start | bytes 2654208 | tf_op jit(solution)/shard_map/reduce_scatter | solution.py:356
  718.8 120.7 %reduce-scatter.11.cloned.1.call-start = ((), (), s32[]{:S(2)}) async-start(), calls=%async_computation.21 | async-start | bytes 2654208 | tf_op jit(solution)/shard_map/reduce_scatter | solution.py:357
  773.8 1.3 copy-start.2
  785.9 123.9 %reduce-scatter.15.cloned.1.call-start = ((), (), s32[]{:S(2)}) async-start(), calls=%async_computation.23 | async-start | bytes 10616832 | tf_op jit(solution)/shard_map/reduce_scatter | solution.py:363
  795.0 194.7 %reduce-scatter.17.cloned.1.call-start = ((), (), s32[]{:S(2)}) async-start(), calls=%async_computation.24 | async-start | bytes 10616832 | tf_op jit(solution)/shard_map/reduce_scatter | solution.py:365
  805.6 1.6 copy-start.31
  805.6 266.3 %all-reduce.23.cloned.1.call-start = ((), (), s32[]{:S(2)}) async-start(), calls=%async_computation.25 | async-start | bytes 3538944 | tf_op jit(solution)/shard_map/psum | solution.py:387
  817.9 7.0 copy-start.3
  841.1 150.7 %copy-start.12 = (bf16[768,768]{1,0:T(8,128)(2,1)S(1)}, bf16[768,768]{1,0:T(8,128)(2,1)}, u32[]{:S(2)}) copy-start(bf16[768,768]{1,0:T(8,128)(2,1)} %reshape.324) | copy-start | bytes 3538948
  841.1 150.7 %copy-start.37 = (bf16[768,768]{1,0:T(8,128)(2,1)S(1)}, bf16[768,768]{1,0:T(8,128)(2,1)}, u32[]{:S(2)}) copy-start(bf16[768,768]{1,0:T(8,128)(2,1)} %all-gather.10.cloned.1.call-done) | copy-start | bytes 3538948
  991.9 1.3 copy-start.13
  991.9 1.3 copy-start.21
  991.9 1.3 copy-start.24
  991.9 1.2 copy-start.26
  991.9 1.6 copy-start.36
  991.9 2.4 copy-start.39
  994.3 3.8 copy-start.29
  994.3 65.9 %copy-start.6 = (f32[768,768]{1,0:T(8,128)S(1)}, f32[768,768]{1,0:T(8,128)}, u32[]{:S(2)}) copy-start(f32[768,768]{1,0:T(8,128)} %copy-done.5) | copy-start | bytes 7077892
  1071.9 4.4 copy-start.19
  1071.9 5.1 copy-start.18
  1071.9 5.9 copy-start.17
  1071.9 6.6 copy-start.16
  (5 other events, 3.8 us)
Sparse Core Ops, SparseCore 0:
  9.9 26.8 all-gather.11
  38.7 24.0 all-gather.9
  64.7 24.0 all-gather.7
  90.5 24.0 all-gather.13
  119.5 40.9 all-gather.15
  305.0 41.7 all-gather.17
  416.9 46.0 reduce-scatter.12
  652.4 43.7 reduce-scatter.6
  718.9 43.6 reduce-scatter.8
  786.0 43.7 reduce-scatter.10
  833.3 76.4 reduce-scatter.14
  913.1 76.4 reduce-scatter.16
  993.7 78.2 all-reduce.22
